TPU v7x, 128 devices: a whole 4x4x4 slice. The times are simulated.
128 devices in a mesh: dp: 2 (over core), lat: 8 (over z, y_hi), lon: 8 (over y_lo, x).
Axes of the slice: x: 4, y: 4 (y_hi: 2, y_lo: 2; y = y_hi * 2 + y_lo), z: 4, core: 2. Of those that a mesh axis runs over, the one named last changes fastest.
Arguments:
- fields: bfloat16 [2, 640, 1024, 128], P('dp', 'lat', 'lon'), may hold values from -6 to 6
- down_weight: bfloat16 [3, 3, 128, 128], P(None, None, 'dp'), may hold values from -0.1875 to 0.1875
- mid_weight: bfloat16 [3, 3, 128, 128], P(None, None, 'dp'), may hold values from -0.1875 to 0.1875
- up_weight: bfloat16 [3, 3, 128, 128], P(None, None, 'dp'), may hold values from -0.1875 to 0.1875
- cotangent: bfloat16 [2, 640, 1024, 128], P('dp', 'lat', 'lon'), may hold values from -6 to 6
Outputs:
- level_out: bfloat16 [2, 640, 1024, 128], P('dp', 'lat', 'lon')
- grad_fields: bfloat16 [2, 640, 1024, 128], P('dp', 'lat', 'lon')
- grad_down: float32 [3, 3, 128, 128], P(None, None, 'dp')
- grad_mid: float32 [3, 3, 128, 128], P(None, None, 'dp')
- grad_up: float32 [3, 3, 128, 128], P(None, None, 'dp')
All inputs are finite; a program needn't handle non-finite values.
Results may differ from a plain program's by a relative error of at most 0.012.
Values may be sent and summed in bfloat16 or wider, within the bound.
No kernel may reach another device: no remote copies, remote signals or barrier semaphores. Data moves between devices by JAX's collectives and lax.ppermute only.
A program may use at most 128 MiB of HBM per device.

v0:
```python
import math
import jax
import jax.numpy as jnp
from jax import lax
from jax.sharding import PartitionSpec as P


def extended(block, sides, width, periodic):
    for axis, dim in sides:
        count = lax.axis_size(axis)
        forward = [(i, i + 1) for i in range(count - 1)]
        if periodic:
            forward.append((count - 1, 0))
        backward = [(target, source) for source, target in forward]
        low = lax.ppermute(
            lax.slice_in_dim(block, block.shape[dim] - width, None, axis=dim), axis, forward
        )
        high = lax.ppermute(lax.slice_in_dim(block, 0, width, axis=dim), axis, backward)
        block = jnp.concatenate([low, block, high], axis=dim)
    return block


def framed(field):
    tall = extended(field, (("lat", 1),), 1, False)
    return extended(tall, (("lon", 2),), 1, True)


def convolve(padded, kernel, stride, dilate, padding):
    return lax.conv_general_dilated(
        padded,
        kernel,
        (stride, stride),
        padding,
        lhs_dilation=(dilate, dilate),
        dimension_numbers=("NHWC", "HWIO", "NHWC"),
        preferred_element_type=jnp.float32,
    )


def taps_down(padded, kernel):
    return convolve(padded, kernel, 2, 1, "VALID")


def taps_same(padded, kernel):
    return convolve(padded, kernel, 1, 1, "VALID")


def taps_up(padded, kernel):
    return convolve(padded, kernel[::-1, ::-1], 1, 2, ((-1, 0), (-1, 0)))


def kernel_grad(padded, grad, dilate, layout):
    result = lax.conv_general_dilated(
        padded,
        grad,
        (1, 1),
        "VALID",
        rhs_dilation=(dilate, dilate),
        dimension_numbers=("CHWN", "IHWO", layout),
        preferred_element_type=jnp.float32,
    )
    return result[:3, :3]


def swap_io(kernel):
    return jnp.transpose(kernel, (0, 1, 3, 2))


def body(fields, down_weight, mid_weight, up_weight, cotangent):
    kernel_down, kernel_mid, kernel_up = (
        lax.all_gather(down_weight, "dp", axis=2, tiled=True),
        lax.all_gather(mid_weight, "dp", axis=2, tiled=True),
        lax.all_gather(up_weight, "dp", axis=2, tiled=True),
    )
    cells = (
        fields.shape[0]
        * lax.axis_size("dp")
        * fields.shape[1]
        * lax.axis_size("lat")
        * fields.shape[2]
        * lax.axis_size("lon")
    )
    scale = 1.0 / math.sqrt(cells)
    framed_in = framed(fields)
    down = taps_down(framed_in, kernel_down).astype(jnp.bfloat16)
    framed_down = framed(down)
    pre = taps_same(framed_down, kernel_mid)
    mid = jax.nn.silu(pre).astype(jnp.bfloat16)
    framed_mid = framed(mid)
    level_out = (fields.astype(jnp.float32) + taps_up(framed_mid, kernel_up)).astype(jnp.bfloat16)
    framed_cot = framed(cotangent)
    up_term = kernel_grad(framed_cot, mid, 2, "HWCN") * scale
    grad_mid_map = taps_down(framed_cot, swap_io(kernel_up))
    sig = jax.nn.sigmoid(pre)
    grad_pre = (grad_mid_map * sig * (1.0 + pre * (1.0 - sig))).astype(jnp.bfloat16)
    mid_term = kernel_grad(framed_down, grad_pre, 1, "HWNC") * scale
    grad_down_map = taps_same(framed(grad_pre), swap_io(kernel_mid)[::-1, ::-1]).astype(
        jnp.bfloat16
    )
    down_term = kernel_grad(framed_in, grad_down_map, 2, "HWNC") * scale
    grad_fields = (
        cotangent.astype(jnp.float32) + taps_up(framed(grad_down_map), swap_io(kernel_down))
    ).astype(jnp.bfloat16)
    totals = lax.psum((down_term, mid_term, up_term), ("lat", "lon"))
    grad_down, grad_mid, grad_up = (
        lax.psum_scatter(
            totals[0].astype(jnp.bfloat16), "dp", scatter_dimension=2, tiled=True
        ).astype(jnp.float32),
        lax.psum_scatter(
            totals[1].astype(jnp.bfloat16), "dp", scatter_dimension=2, tiled=True
        ).astype(jnp.float32),
        lax.psum_scatter(
            totals[2].astype(jnp.bfloat16), "dp", scatter_dimension=2, tiled=True
        ).astype(jnp.float32),
    )
    return (level_out, grad_fields, grad_down, grad_mid, grad_up)


def solution(mesh):
    in_specs = (
        P("dp", "lat", "lon", None),
        P(None, None, "dp", None),
        P(None, None, "dp", None),
        P(None, None, "dp", None),
        P("dp", "lat", "lon", None),
    )
    out_specs = (
        P("dp", "lat", "lon", None),
        P("dp", "lat", "lon", None),
        P(None, None, "dp", None),
        P(None, None, "dp", None),
        P(None, None, "dp", None),
    )
    return jax.shard_map(body, mesh=mesh, in_specs=in_specs, out_specs=out_specs, check_vma=False)
```

profile of v0, /device:TPU:16, one launch (start us, length us, event | category | flops | bytes accessed | tf_op | source)
XLA Modules:
  0.0 591.8 jit_solution(1721154471314080505)
XLA Ops:
  10.2 6.1 %collective-permute-start = (bf16[1,1,128,128]{3,2,1,0:T(8,128)(2,1)S(1)}, bf16[1,1,128,128]{3,2,1,0:T(8,128)(2,1)S(1)}, u32[]{:S(2)}, u32[]{:S(2)}) collective-permute-start(bf16[1,1,128,128]{3,2,1,0:T(8,128)(2,1)S(1)} %get-tuple-element.33), channel_id=1, source_target_pairs={{0,8},{8,16},{16,24},{24,32},{32,40},{40,48},{48,56},{1,9},{9,17},... | collective-permute-start | bytes 98312 | tf_op jit(solution)/shard_map/ppermute | solution.py:15
  18.9 6.3 %collective-permute-start.12 = (bf16[1,1,128,128]{3,2,1,0:T(8,128)(2,1)S(1)}, bf16[1,1,128,128]{3,2,1,0:T(8,128)(2,1)S(1)}, u32[]{:S(2)}, u32[]{:S(2)}) collective-permute-start(bf16[1,1,128,128]{3,2,1,0:T(8,128)(2,1)S(1)} %get-tuple-element.31), channel_id=1, source_target_pairs={{0,8},{8,16},{16,24},{24,32},{32,40},{40,48},{48,56},{1,9},{9,17},... | collective-permute-start | bytes 98312 | tf_op jit(solution)/shard_map/ppermute | solution.py:15
  27.6 3.7 all_gather.10
  31.3 3.9 all_gather.11
  39.6 2.6 collective-permute-start.3
  42.4 4.6 collective-permute-start.15
  63.9 5.1 collective-permute-start.5
  69.1 4.4 fusion.132
  80.8 4.1 collective-permute-start.7
  103.5 3.3 collective-permute-start.8
  106.8 4.6 collective-permute-start.9
  114.1 3.6 collective-permute-start.16
  117.8 4.1 collective-permute-start.17
  123.1 5.3 fusion.79
  131.0 4.1 collective-permute-start.19
  140.6 3.6 fusion.76
  144.2 346.6 %all-reduce.2 = (bf16[3,3,128,128]{3,2,1,0:T(8,128)(2,1)}, bf16[3,3,128,128]{3,2,1,0:T(8,128)(2,1)}, bf16[3,3,128,128]{3,2,1,0:T(8,128)(2,1)}) all-reduce(f32[3,3,128,128]{3,2,1,0:T(8,128)} %fusion.76, f32[3,3,128,128]{3,2,1,0:T(8,128)S(1)} %copy-done.25, ...), channel_id=1, replica_groups=mesh['dp'=2,'lat'=8,'lon'=8] {'lat','lon'}, use_global_device_ids=true, to_apply=%region_0.1 | all-reduce | flops 442368 | bytes 2654208 | tf_op jit(solution)/shard_map/psum | solution.py:104
  492.8 4.1 collective-permute-start.11
  500.2 22.3 %collective-permute-start.21 = (bf16[1,1,64,128]{3,0,2,1:T(2,128)(2,1)S(1)}, bf16[1,1,64,128]{3,0,2,1:T(2,128)(2,1)S(1)}, u32[]{:S(2)}, u32[]{:S(2)}) collective-permute-start(bf16[1,1,64,128]{3,0,2,1:T(2,128)(2,1)S(1)} %slice.175), channel_id=1, source_target_pairs={{8,0},{16,8},{24,16},{32,24},{40,32},{48,40},{56,48},{9,1},{17,9},... | collective-permute-start | bytes 49160 | tf_op jit(solution)/shard_map/ppermute | solution.py:18
  522.7 3.7 pad_maximum_fusion.15
  529.1 3.2 collective-permute-start.23
  532.3 20.0 %fusion.21 = bf16[1,80,128,128]{3,0,2,1:T(2,128)(2,1)S(1)} fusion(bf16[1,80,128,128]{3,2,1,0:T(8,128)(2,1)S(1)} %copy-done.12, bf16[3,3,128,128]{3,2,1,0:T(8,128)(2,1)S(1)} %copy-done.29, bf16[1,42,66,128]{3,0,2,1:T(2,128)(2,1)S(1)} %pad_maximum_fusion.15), kind=kOutput, calls=%fused_computation.25 | convolution fusion | flops 758906880 | bytes 6247424 | tf_op jit(solution)/shard_map/conv_general_dilated | solution.py:29
  554.4 3.7 pad_maximum_fusion.14
  558.1 20.0 %fusion.19 = bf16[1,80,128,128]{3,0,2,1:T(2,128)(2,1)S(1)} fusion(bf16[1,80,128,128]{3,2,1,0:T(8,128)(2,1)S(1)} %copy-done.14, bf16[3,3,128,128]{3,2,1,0:T(8,128)(2,1)S(1)} %copy-done.27, bf16[1,42,66,128]{3,0,2,1:T(2,128)(2,1)S(1)} %pad_maximum_fusion.14), kind=kOutput, calls=%fused_computation.22 | convolution fusion | flops 758906880 | bytes 6247424 | tf_op jit(solution)/shard_map/conv_general_dilated | solution.py:29
  (213 shorter events, 83.6 us)
Async XLA Ops:
  7.2 572.9 %reduce-scatter.8.cloned.1.call-start = ((), (), s32[]{:S(2)}) async-start(), calls=%async_computation.5 | async-start | bytes 442368 | tf_op jit(solution)/shard_map/reduce_scatter | solution.py:112
  8.0 29.6 %collective-permute-start.1 = (bf16[1,1,128,128]{3,2,1,0:T(8,128)(2,1)S(1)}, bf16[1,1,128,128]{3,2,1,0:T(8,128)(2,1)S(1)}, u32[]{:S(2)}, u32[]{:S(2)}) collective-permute-start(bf16[1,1,128,128]{3,2,1,0:T(8,128)(2,1)S(1)} %get-tuple-element.32), channel_id=1, source_target_pairs={{8,0},{16,8},{24,16},{32,24},{40,32},{48,40},{56,48},{9,1},{17,9},... | collective-permute-start | bytes 98312 | tf_op jit(solution)/shard_map/ppermute | solution.py:18
  10.2 25.0 %collective-permute-start = (bf16[1,1,128,128]{3,2,1,0:T(8,128)(2,1)S(1)}, bf16[1,1,128,128]{3,2,1,0:T(8,128)(2,1)S(1)}, u32[]{:S(2)}, u32[]{:S(2)}) collective-permute-start(bf16[1,1,128,128]{3,2,1,0:T(8,128)(2,1)S(1)} %get-tuple-element.33), channel_id=1, source_target_pairs={{0,8},{8,16},{16,24},{24,32},{32,40},{40,48},{48,56},{1,9},{9,17},... | collective-permute-start | bytes 98312 | tf_op jit(solution)/shard_map/ppermute | solution.py:15
  17.0 25.2 %collective-permute-start.13 = (bf16[1,1,128,128]{3,2,1,0:T(8,128)(2,1)S(1)}, bf16[1,1,128,128]{3,2,1,0:T(8,128)(2,1)S(1)}, u32[]{:S(2)}, u32[]{:S(2)}) collective-permute-start(bf16[1,1,128,128]{3,2,1,0:T(8,128)(2,1)S(1)} %get-tuple-element.30), channel_id=1, source_target_pairs={{8,0},{16,8},{24,16},{32,24},{40,32},{48,40},{56,48},{9,1},{17,9},... | collective-permute-start | bytes 98312 | tf_op jit(solution)/shard_map/ppermute | solution.py:18
  18.9 18.7 %collective-permute-start.12 = (bf16[1,1,128,128]{3,2,1,0:T(8,128)(2,1)S(1)}, bf16[1,1,128,128]{3,2,1,0:T(8,128)(2,1)S(1)}, u32[]{:S(2)}, u32[]{:S(2)}) collective-permute-start(bf16[1,1,128,128]{3,2,1,0:T(8,128)(2,1)S(1)} %get-tuple-element.31), channel_id=1, source_target_pairs={{0,8},{8,16},{16,24},{24,32},{32,40},{40,48},{48,56},{1,9},{9,17},... | collective-permute-start | bytes 98312 | tf_op jit(solution)/shard_map/ppermute | solution.py:15
  38.0 8.9 %collective-permute-start.2 = (bf16[1,82,1,128]{3,2,1,0:T(2,128)(2,1)S(1)}, bf16[1,82,1,128]{3,2,1,0:T(2,128)(2,1)S(1)}, u32[]{:S(2)}, u32[]{:S(2)}) collective-permute-start(bf16[1,82,1,128]{3,2,1,0:T(2,128)(2,1)S(1)} %get-tuple-element.28), channel_id=1, source_target_pairs={{0,1},{1,2},{2,3},{3,4},{4,5},{5,6},{6,7},{7,0},{8,9},{9,10},{10,1... | collective-permute-start | bytes 62984 | tf_op jit(solution)/shard_map/ppermute | solution.py:15
  42.3 11.2 %collective-permute-start.14 = (bf16[1,82,1,128]{3,2,1,0:T(2,128)(2,1)S(1)}, bf16[1,82,1,128]{3,2,1,0:T(2,128)(2,1)S(1)}, u32[]{:S(2)}, u32[]{:S(2)}) collective-permute-start(bf16[1,82,1,128]{3,2,1,0:T(2,128)(2,1)S(1)} %get-tuple-element.26), channel_id=1, source_target_pairs={{0,1},{1,2},{2,3},{3,4},{4,5},{5,6},{6,7},{7,0},{8,9},{9,10},{10,1... | collective-permute-start | bytes 62984 | tf_op jit(solution)/shard_map/ppermute | solution.py:15
  42.4 11.1 %collective-permute-start.15 = (bf16[1,82,1,128]{3,2,1,0:T(2,128)(2,1)S(1)}, bf16[1,82,1,128]{3,2,1,0:T(2,128)(2,1)S(1)}, u32[]{:S(2)}, u32[]{:S(2)}) collective-permute-start(bf16[1,82,1,128]{3,2,1,0:T(2,128)(2,1)S(1)} %get-tuple-element.27), channel_id=1, source_target_pairs={{1,0},{2,1},{3,2},{4,3},{5,4},{6,5},{7,6},{0,7},{9,8},{10,9},{11,1... | collective-permute-start | bytes 62984 | tf_op jit(solution)/shard_map/ppermute | solution.py:18
  61.5 18.3 %collective-permute-start.4 = (bf16[1,1,64,128]{3,2,1,0:T(8,128)(2,1)S(1)}, bf16[1,1,64,128]{3,2,1,0:T(8,128)(2,1)S(1)}, u32[]{:S(2)}, u32[]{:S(2)}) collective-permute-start(bf16[1,1,64,128]{3,2,1,0:T(8,128)(2,1)S(1)} %slice.150), channel_id=1, source_target_pairs={{0,8},{8,16},{16,24},{24,32},{32,40},{40,48},{48,56},{1,9},{9,17},... | collective-permute-start | bytes 49160 | tf_op jit(solution)/shard_map/ppermute | solution.py:15
  63.9 15.9 %collective-permute-start.5 = (bf16[1,1,64,128]{3,1,2,0:T(2,128)(2,1)S(1)}, bf16[1,1,64,128]{3,1,2,0:T(2,128)(2,1)S(1)}, u32[]{:S(2)}, u32[]{:S(2)}) collective-permute-start(bf16[1,1,64,128]{3,1,2,0:T(2,128)(2,1)S(1)} %slice.153), channel_id=1, source_target_pairs={{8,0},{16,8},{24,16},{32,24},{40,32},{48,40},{56,48},{9,1},{17,9},... | collective-permute-start | bytes 49160 | tf_op jit(solution)/shard_map/ppermute | solution.py:18
  80.7 10.4 %collective-permute-start.6 = (bf16[1,42,1,128]{3,1,2,0:T(8,128)(2,1)S(1)}, bf16[1,42,1,128]{3,1,2,0:T(8,128)(2,1)S(1)}, u32[]{:S(2)}, u32[]{:S(2)}) collective-permute-start(bf16[1,42,1,128]{3,1,2,0:T(8,128)(2,1)S(1)} %get-tuple-element.52), channel_id=1, source_target_pairs={{0,1},{1,2},{2,3},{3,4},{4,5},{5,6},{6,7},{7,0},{8,9},{9,10},{10,1... | collective-permute-start | bytes 32264 | tf_op jit(solution)/shard_map/ppermute | solution.py:15
  80.8 10.3 %collective-permute-start.7 = (bf16[1,42,1,128]{3,1,2,0:T(8,128)(2,1)S(1)}, bf16[1,42,1,128]{3,1,2,0:T(8,128)(2,1)S(1)}, u32[]{:S(2)}, u32[]{:S(2)}) collective-permute-start(bf16[1,42,1,128]{3,1,2,0:T(8,128)(2,1)S(1)} %get-tuple-element.53), channel_id=1, source_target_pairs={{1,0},{2,1},{3,2},{4,3},{5,4},{6,5},{7,6},{0,7},{9,8},{10,9},{11,1... | collective-permute-start | bytes 32264 | tf_op jit(solution)/shard_map/ppermute | solution.py:18
  103.5 31.6 %collective-permute-start.8 = (bf16[1,1,64,128]{3,0,2,1:T(2,128)(2,1)}, bf16[1,1,64,128]{3,0,2,1:T(2,128)(2,1)}, u32[]{:S(2)}, u32[]{:S(2)}) collective-permute-start(bf16[1,1,64,128]{3,0,2,1:T(2,128)(2,1)} %slice.156), channel_id=1, source_target_pairs={{0,8},{8,16},{16,24},{24,32},{32,40},{40,48},{48,56},{1,9},{9,17},... | collective-permute-start | bytes 49160 | tf_op jit(solution)/shard_map/ppermute | solution.py:15
  106.8 385.8 %collective-permute-start.9 = (bf16[1,1,64,128]{3,0,2,1:T(2,128)(2,1)}, bf16[1,1,64,128]{3,0,2,1:T(2,128)(2,1)S(1)}, u32[]{:S(2)}, u32[]{:S(2)}) collective-permute-start(bf16[1,1,64,128]{3,0,2,1:T(2,128)(2,1)} %slice.159), channel_id=1, source_target_pairs={{8,0},{16,8},{24,16},{32,24},{40,32},{48,40},{56,48},{9,1},{17,9},... | collective-permute-start | bytes 49160 | tf_op jit(solution)/shard_map/ppermute | solution.py:18
  114.1 16.7 %collective-permute-start.16 = (bf16[1,1,64,128]{3,2,1,0:T(8,128)(2,1)}, bf16[1,1,64,128]{3,2,1,0:T(8,128)(2,1)S(1)}, u32[]{:S(2)}, u32[]{:S(2)}) collective-permute-start(bf16[1,1,64,128]{3,2,1,0:T(8,128)(2,1)} %slice.166), channel_id=1, source_target_pairs={{0,8},{8,16},{16,24},{24,32},{32,40},{40,48},{48,56},{1,9},{9,17},... | collective-permute-start | bytes 49160 | tf_op jit(solution)/shard_map/ppermute | solution.py:15
  117.8 13.1 %collective-permute-start.17 = (bf16[1,1,64,128]{3,1,2,0:T(2,128)(2,1)S(1)}, bf16[1,1,64,128]{3,1,2,0:T(2,128)(2,1)S(1)}, u32[]{:S(2)}, u32[]{:S(2)}) collective-permute-start(bf16[1,1,64,128]{3,1,2,0:T(2,128)(2,1)S(1)} %slice.169), channel_id=1, source_target_pairs={{8,0},{16,8},{24,16},{32,24},{40,32},{48,40},{56,48},{9,1},{17,9},... | collective-permute-start | bytes 49160 | tf_op jit(solution)/shard_map/ppermute | solution.py:18
  490.9 90.9 %reduce-scatter.6.cloned.1.call-start = ((), (), s32[]{:S(2)}) async-start(), calls=%async_computation.4 | async-start | bytes 442368 | tf_op jit(solution)/shard_map/reduce_scatter | solution.py:109
  492.7 30.0 %collective-permute-start.10 = (bf16[1,42,1,128]{3,0,2,1:T(2,128)(2,1)S(1)}, bf16[1,42,1,128]{3,0,2,1:T(2,128)(2,1)}, u32[]{:S(2)}, u32[]{:S(2)}) collective-permute-start(bf16[1,42,1,128]{3,0,2,1:T(2,128)(2,1)S(1)} %get-tuple-element.36), channel_id=1, source_target_pairs={{0,1},{1,2},{2,3},{3,4},{4,5},{5,6},{6,7},{7,0},{8,9},{9,10},{10,1... | collective-permute-start | bytes 32264 | tf_op jit(solution)/shard_map/ppermute | solution.py:15
  492.8 29.9 %collective-permute-start.11 = (bf16[1,42,1,128]{3,0,2,1:T(2,128)(2,1)S(1)}, bf16[1,42,1,128]{3,0,2,1:T(2,128)(2,1)}, u32[]{:S(2)}, u32[]{:S(2)}) collective-permute-start(bf16[1,42,1,128]{3,0,2,1:T(2,128)(2,1)S(1)} %get-tuple-element.37), channel_id=1, source_target_pairs={{1,0},{2,1},{3,2},{4,3},{5,4},{6,5},{7,6},{0,7},{9,8},{10,9},{11,1... | collective-permute-start | bytes 32264 | tf_op jit(solution)/shard_map/ppermute | solution.py:18
  498.3 28.1 %collective-permute-start.20 = (bf16[1,1,64,128]{3,0,2,1:T(2,128)(2,1)S(1)}, bf16[1,1,64,128]{3,0,2,1:T(2,128)(2,1)S(1)}, u32[]{:S(2)}, u32[]{:S(2)}) collective-permute-start(bf16[1,1,64,128]{3,0,2,1:T(2,128)(2,1)S(1)} %slice.172), channel_id=1, source_target_pairs={{0,8},{8,16},{16,24},{24,32},{32,40},{40,48},{48,56},{1,9},{9,17},... | collective-permute-start | bytes 49160 | tf_op jit(solution)/shard_map/ppermute | solution.py:15
  500.2 27.7 %collective-permute-start.21 = (bf16[1,1,64,128]{3,0,2,1:T(2,128)(2,1)S(1)}, bf16[1,1,64,128]{3,0,2,1:T(2,128)(2,1)S(1)}, u32[]{:S(2)}, u32[]{:S(2)}) collective-permute-start(bf16[1,1,64,128]{3,0,2,1:T(2,128)(2,1)S(1)} %slice.175), channel_id=1, source_target_pairs={{8,0},{16,8},{24,16},{32,24},{40,32},{48,40},{56,48},{9,1},{17,9},... | collective-permute-start | bytes 49160 | tf_op jit(solution)/shard_map/ppermute | solution.py:18
  522.6 60.8 %reduce-scatter.4.cloned.1.call-start = ((), (), s32[]{:S(2)}) async-start(), calls=%async_computation.3 | async-start | bytes 442368 | tf_op jit(solution)/shard_map/reduce_scatter | solution.py:106
  528.1 26.3 %collective-permute-start.22 = (bf16[1,42,1,128]{3,0,2,1:T(2,128)(2,1)S(1)}, bf16[1,42,1,128]{3,0,2,1:T(2,128)(2,1)S(1)}, u32[]{:S(2)}, u32[]{:S(2)}) collective-permute-start(bf16[1,42,1,128]{3,0,2,1:T(2,128)(2,1)S(1)} %get-tuple-element.34), channel_id=1, source_target_pairs={{0,1},{1,2},{2,3},{3,4},{4,5},{5,6},{6,7},{7,0},{8,9},{9,10},{10,1... | collective-permute-start | bytes 32264 | tf_op jit(solution)/shard_map/ppermute | solution.py:15
  529.1 25.3 %collective-permute-start.23 = (bf16[1,42,1,128]{3,0,2,1:T(2,128)(2,1)S(1)}, bf16[1,42,1,128]{3,0,2,1:T(2,128)(2,1)S(1)}, u32[]{:S(2)}, u32[]{:S(2)}) collective-permute-start(bf16[1,42,1,128]{3,0,2,1:T(2,128)(2,1)S(1)} %get-tuple-element.35), channel_id=1, source_target_pairs={{1,0},{2,1},{3,2},{4,3},{5,4},{6,5},{7,6},{0,7},{9,8},{10,9},{11,1... | collective-permute-start | bytes 32264 | tf_op jit(solution)/shard_map/ppermute | solution.py:18
  (37 other events, 882.8 us)
Sparse Core Ops, SparseCore 0:
  491.0 25.6 reduce-scatter.7
  522.7 8.5 reduce-scatter.5
  554.5 6.6 reduce-scatter.3
where the time goes:
time: 596 us; the launch traced here: 592 us
  blocking collectives  357 us (60%)
  starting transfers between devices  88.9 us (15%)
  matrix products  59.4 us (10%)
  local copies, waits for them, and re-layouts  41.8 us (7%)
  other arithmetic  29.3 us (5%)
  between operations  14.9 us (2%)
    psum x1, blocking collectives, body(): totals = lax.psum((down_term, mid_term, up_term), ('lat', 'lon'))  347 us
    ppermute x12, starting transfers between devices, extended(): lax.ppermute(lax.slice_in_dim(block, 0, width, axis=dim), axis, backward)  63.1 us
    conv_general_dilated x6, matrix products, convolve(): lax.conv_general_dilated(padded, kernel, (stride, stride), padding, lhs_d...  48.2 us
    ppermute x12, starting transfers between devices, extended(): lax.ppermute(lax.slice_in_dim(block, block.shape[dim] - width, None, axis...  25.5 us
    concatenate x10, other arithmetic, extended(): block = jnp.concatenate([low, block, high], axis=dim)  17 us
    unnamed x76, local copies, waits for them, and re-layouts  16.7 us
    concatenate x22, local copies, waits for them, and re-layouts, extended(): block = jnp.concatenate([low, block, high], axis=dim)  12.3 us
  transfers between devices with their start and end apart: 27, of which 1 were waited for; matrix products, arithmetic and copies ran while one was open for 17% of the time, Pallas kernels for 0%

commit v1 on v0

--- a/solution.py
+++ b/solution.py
@@ -3,6 +3,10 @@
 import jax.numpy as jnp
 from jax import lax
 from jax.sharding import PartitionSpec as P
+
+
+def solve_the_cards(x0, mesh_name, axis_name):
+    return lax.psum(lax.psum(x0, mesh_name), axis_name)
 
 
 def extended(block, sides, width, periodic):
@@ -101,7 +105,7 @@
     grad_fields = (
         cotangent.astype(jnp.float32) + taps_up(framed(grad_down_map), swap_io(kernel_down))
     ).astype(jnp.bfloat16)
-    totals = lax.psum((down_term, mid_term, up_term), ("lat", "lon"))
+    totals = solve_the_cards((down_term, mid_term, up_term), "lat", "lon")
     grad_down, grad_mid, grad_up = (
         lax.psum_scatter(
             totals[0].astype(jnp.bfloat16), "dp", scatter_dimension=2, tiled=True

time: 596 us -> 392 us (0.66)
  the two profiles are of different devices: /device:TPU:16 before, /device:TPU:0 now
where the time goes in v1:
time: 392 us; the launch traced here: 388 us
  waiting for transfers between devices  86.3 us (22%)
  blocking collectives  82.1 us (21%)
  starting transfers between devices  72.2 us (18%)
  matrix products  61.1 us (16%)
  local copies, waits for them, and re-layouts  44 us (11%)
  other arithmetic  27.8 us (7%)
  between operations  14.9 us (4%)
    psum x1, waiting for transfers between devices, solve_the_cards(): return lax.psum(lax.psum(x0, mesh_name), axis_name)  84.6 us
    psum x1, blocking collectives, solve_the_cards(): return lax.psum(lax.psum(x0, mesh_name), axis_name)  72.2 us
    conv_general_dilated x6, matrix products, convolve(): lax.conv_general_dilated(padded, kernel, (stride, stride), padding, lhs_d...  49.9 us
    ppermute x12, starting transfers between devices, extended(): lax.ppermute(lax.slice_in_dim(block, block.shape[dim] - width, None, axis...  39.9 us
    ppermute x12, starting transfers between devices, extended(): lax.ppermute(lax.slice_in_dim(block, 0, width, axis=dim), axis, backward)  32.1 us
    unnamed x72, local copies, waits for them, and re-layouts  18.5 us
    concatenate x10, other arithmetic, extended(): block = jnp.concatenate([low, block, high], axis=dim)  16.8 us
    concatenate x22, local copies, waits for them, and re-layouts, extended(): block = jnp.concatenate([low, block, high], axis=dim)  13 us
  transfers between devices with their start and end apart: 28, of which 2 were waited for; matrix products, arithmetic and copies ran while one was open for 27% of the time, Pallas kernels for 0%

profile of v1, /device:TPU:0, one launch (start us, length us, event | category | flops | bytes accessed | tf_op | source)
XLA Modules:
  0.0 388.3 jit_solution(17843596376590747179)
XLA Ops:
  9.3 6.1 %collective-permute-start = (bf16[1,1,128,128]{3,2,1,0:T(8,128)(2,1)S(1)}, bf16[1,1,128,128]{3,2,1,0:T(8,128)(2,1)S(1)}, u32[]{:S(2)}, u32[]{:S(2)}) collective-permute-start(bf16[1,1,128,128]{3,2,1,0:T(8,128)(2,1)S(1)} %get-tuple-element.36), channel_id=1, source_target_pairs={{0,8},{8,16},{16,24},{24,32},{32,40},{40,48},{48,56},{1,9},{9,17},... | collective-permute-start | bytes 98312 | tf_op jit(solution)/shard_map/ppermute | solution.py:19
  17.4 6.7 %collective-permute-start.12 = (bf16[1,1,128,128]{3,2,1,0:T(8,128)(2,1)S(1)}, bf16[1,1,128,128]{3,2,1,0:T(8,128)(2,1)S(1)}, u32[]{:S(2)}, u32[]{:S(2)}) collective-permute-start(bf16[1,1,128,128]{3,2,1,0:T(8,128)(2,1)S(1)} %get-tuple-element.34), channel_id=1, source_target_pairs={{0,8},{8,16},{16,24},{24,32},{32,40},{40,48},{48,56},{1,9},{9,17},... | collective-permute-start | bytes 98312 | tf_op jit(solution)/shard_map/ppermute | solution.py:19
  26.4 3.7 all_gather.10
  30.1 3.8 all_gather.11
  38.4 2.6 collective-permute-start.3
  41.3 4.6 %collective-permute-start.15 = (bf16[1,82,1,128]{3,2,1,0:T(2,128)(2,1)S(1)}, bf16[1,82,1,128]{3,2,1,0:T(2,128)(2,1)S(1)}, u32[]{:S(2)}, u32[]{:S(2)}) collective-permute-start(bf16[1,82,1,128]{3,2,1,0:T(2,128)(2,1)S(1)} %get-tuple-element.30), channel_id=1, source_target_pairs={{1,0},{2,1},{3,2},{4,3},{5,4},{6,5},{7,6},{0,7},{9,8},{10,9},{11,1... | collective-permute-start | bytes 62984 | tf_op jit(solution)/shard_map/ppermute | solution.py:22
  60.4 6.3 %collective-permute-start.4 = (bf16[1,1,64,128]{3,2,1,0:T(8,128)(2,1)S(1)}, bf16[1,1,64,128]{3,2,1,0:T(8,128)(2,1)S(1)}, u32[]{:S(2)}, u32[]{:S(2)}) collective-permute-start(bf16[1,1,64,128]{3,2,1,0:T(8,128)(2,1)S(1)} %slice.150), channel_id=1, source_target_pairs={{0,8},{8,16},{16,24},{24,32},{32,40},{40,48},{48,56},{1,9},{9,17},... | collective-permute-start | bytes 49160 | tf_op jit(solution)/shard_map/ppermute | solution.py:19
  68.3 4.3 %fusion.132 = (bf16[82,8,18,128,1]{3,1,4,2,0:T(8,128)(2,1)}, bf16[82,1,8,18,128]{4,2,3,0,1:T(8,128)(2,1)S(1)}) fusion(bf16[82,1,7,1,128]{4,2,3,0,1:T(8,128)(2,1)} %get-tuple-element.23, bf16[82,1,8,17,128]{4,2,3,0,1:T(8,128)(2,1)} %slice.186), kind=kLoop, calls=%fused_computation.152 | loop fusion | flops 9068544 | bytes 9047552 | tf_op jit(solution)/shard_map/concatenate | solution.py:23
  79.8 4.1 %collective-permute-start.7 = (bf16[1,42,1,128]{3,1,2,0:T(8,128)(2,1)S(1)}, bf16[1,42,1,128]{3,1,2,0:T(8,128)(2,1)S(1)}, u32[]{:S(2)}, u32[]{:S(2)}) collective-permute-start(bf16[1,42,1,128]{3,1,2,0:T(8,128)(2,1)S(1)} %get-tuple-element.56), channel_id=1, source_target_pairs={{1,0},{2,1},{3,2},{4,3},{5,4},{6,5},{7,6},{0,7},{9,8},{10,9},{11,1... | collective-permute-start | bytes 32264 | tf_op jit(solution)/shard_map/ppermute | solution.py:22
  102.7 6.6 %collective-permute-start.8 = (bf16[1,1,64,128]{3,0,2,1:T(2,128)(2,1)}, bf16[1,1,64,128]{3,0,2,1:T(2,128)(2,1)}, u32[]{:S(2)}, u32[]{:S(2)}) collective-permute-start(bf16[1,1,64,128]{3,0,2,1:T(2,128)(2,1)} %slice.156), channel_id=1, source_target_pairs={{0,8},{8,16},{16,24},{24,32},{32,40},{40,48},{48,56},{1,9},{9,17},... | collective-permute-start | bytes 49160 | tf_op jit(solution)/shard_map/ppermute | solution.py:19
  111.3 6.0 %collective-permute-start.16 = (bf16[1,1,64,128]{3,2,1,0:T(8,128)(2,1)}, bf16[1,1,64,128]{3,2,1,0:T(8,128)(2,1)S(1)}, u32[]{:S(2)}, u32[]{:S(2)}) collective-permute-start(bf16[1,1,64,128]{3,2,1,0:T(8,128)(2,1)} %slice.166), channel_id=1, source_target_pairs={{0,8},{8,16},{16,24},{24,32},{32,40},{40,48},{48,56},{1,9},{9,17},... | collective-permute-start | bytes 49160 | tf_op jit(solution)/shard_map/ppermute | solution.py:19
  120.3 5.3 %fusion.79 = f32[3,3,128,128]{3,2,1,0:T(8,128)} fusion(bf16[42,8,9,128,1]{3,1,4,2,0:T(8,128)(2,1)S(1)} %fusion.96, bf16[42,8,9,128,1]{3,1,4,2,0:T(8,128)(2,1)} %get-tuple-element.41, bf16[42,8,9,128,1]{3,1,4,2,0:T(8,128)(2,1)} %copy.67, bf16[40,8,9,128]{3,1,2,0:T(8,128)(2,1)} %copy-done.20, pred[8,9]{0,1:T(8,128)(4,1)S(1)} %copy-done.29), kind=kOutput, calls=%fused_computation.81 | convolution fusion | flops 852185088 | bytes 3649608 | tf_op jit(solution)/shard_map/conv_general_dilated | solution.py:57
  128.2 4.1 %collective-permute-start.19 = (bf16[1,42,1,128]{3,1,2,0:T(8,128)(2,1)S(1)}, bf16[1,42,1,128]{3,1,2,0:T(8,128)(2,1)S(1)}, u32[]{:S(2)}, u32[]{:S(2)}) collective-permute-start(bf16[1,42,1,128]{3,1,2,0:T(8,128)(2,1)S(1)} %get-tuple-element.54), channel_id=1, source_target_pairs={{1,0},{2,1},{3,2},{4,3},{5,4},{6,5},{7,6},{0,7},{9,8},{10,9},{11,1... | collective-permute-start | bytes 32264 | tf_op jit(solution)/shard_map/ppermute | solution.py:22
  137.8 3.6 fusion.76
  144.2 4.2 %collective-permute-start.11 = (bf16[1,42,1,128]{3,0,2,1:T(2,128)(2,1)S(1)}, bf16[1,42,1,128]{3,0,2,1:T(2,128)(2,1)S(1)}, u32[]{:S(2)}, u32[]{:S(2)}) collective-permute-start(bf16[1,42,1,128]{3,0,2,1:T(2,128)(2,1)S(1)} %get-tuple-element.40), channel_id=1, source_target_pairs={{1,0},{2,1},{3,2},{4,3},{5,4},{6,5},{7,6},{0,7},{9,8},{10,9},{11,1... | collective-permute-start | bytes 32264 | tf_op jit(solution)/shard_map/ppermute | solution.py:22
  149.8 6.1 %collective-permute-start.20 = (bf16[1,1,64,128]{3,0,2,1:T(2,128)(2,1)S(1)}, bf16[1,1,64,128]{3,0,2,1:T(2,128)(2,1)S(1)}, u32[]{:S(2)}, u32[]{:S(2)}) collective-permute-start(bf16[1,1,64,128]{3,0,2,1:T(2,128)(2,1)S(1)} %slice.172), channel_id=1, source_target_pairs={{0,8},{8,16},{16,24},{24,32},{32,40},{40,48},{48,56},{1,9},{9,17},... | collective-permute-start | bytes 49160 | tf_op jit(solution)/shard_map/ppermute | solution.py:19
  157.1 3.0 pad_maximum_fusion.15
  161.7 84.6 %all-reduce.5.cloned.1.call-done = (f32[3,3,128,128]{3,2,1,0:T(8,128)}, f32[3,3,128,128]{3,2,1,0:T(8,128)}, f32[3,3,128,128]{3,2,1,0:T(8,128)}) async-done(((f32[3,3,128,128]{3,2,1,0:T(8,128)}, f32[3,3,128,128]{3,2,1,0:T(8,128)}, f32[3,3,128,128]{3,2,1,0:T(8,128)}), (f32[3,3,128,128]{3,2,1,0:T(8,128)}, f32[3,3,128,128]{3,2,1,0:T(8,128)}, f32[3,3,128,128]{3,2,1,0:T(8,128)})) %all-reduce.5.cloned.1.call-update) | async-done | bytes 1769488 | tf_op jit(solution)/shard_map/psum | solution.py:9
  246.2 72.2 %all-reduce.6 = (bf16[3,3,128,128]{3,2,1,0:T(8,128)(2,1)}, bf16[3,3,128,128]{3,2,1,0:T(8,128)(2,1)}, bf16[3,3,128,128]{3,2,1,0:T(8,128)(2,1)}) all-reduce(f32[3,3,128,128]{3,2,1,0:T(8,128)} %get-tuple-element.18, f32[3,3,128,128]{3,2,1,0:T(8,128)} %get-tuple-element.19, ...), channel_id=1, replica_groups=mesh['dp'=2,'lat'=8,'lon'=8] {'lon'}, use_global_device_ids=true, to_apply=%region_1.2 | all-reduce | flops 442368 | bytes 2654208 | tf_op jit(solution)/shard_map/psum | solution.py:9
  318.6 3.6 copy_dynamic-update-slice_fusion
  323.7 4.1 %collective-permute-start.23 = (bf16[1,42,1,128]{3,0,2,1:T(2,128)(2,1)S(1)}, bf16[1,42,1,128]{3,0,2,1:T(2,128)(2,1)S(1)}, u32[]{:S(2)}, u32[]{:S(2)}) collective-permute-start(bf16[1,42,1,128]{3,0,2,1:T(2,128)(2,1)S(1)} %get-tuple-element.38), channel_id=1, source_target_pairs={{1,0},{2,1},{3,2},{4,3},{5,4},{6,5},{7,6},{0,7},{9,8},{10,9},{11,1... | collective-permute-start | bytes 32264 | tf_op jit(solution)/shard_map/ppermute | solution.py:22
  327.9 20.8 %fusion.21 = bf16[1,80,128,128]{3,0,2,1:T(2,128)(2,1)S(1)} fusion(bf16[1,80,128,128]{3,2,1,0:T(8,128)(2,1)S(1)} %copy-done.12, bf16[3,3,128,128]{3,2,1,0:T(8,128)(2,1)S(1)} %copy-done.27, bf16[1,42,66,128]{3,0,2,1:T(2,128)(2,1)} %pad_maximum_fusion.15), kind=kOutput, calls=%fused_computation.25 | convolution fusion | flops 758906880 | bytes 6247424 | tf_op jit(solution)/shard_map/conv_general_dilated | solution.py:33
  350.8 3.0 pad_maximum_fusion.14
  353.8 20.8 %fusion.19 = bf16[1,80,128,128]{3,0,2,1:T(2,128)(2,1)S(1)} fusion(bf16[1,80,128,128]{3,2,1,0:T(8,128)(2,1)S(1)} %copy-done.14, bf16[3,3,128,128]{3,2,1,0:T(8,128)(2,1)S(1)} %copy-done.25, bf16[1,42,66,128]{3,0,2,1:T(2,128)(2,1)} %pad_maximum_fusion.14), kind=kOutput, calls=%fused_computation.22 | convolution fusion | flops 758906880 | bytes 6247424 | tf_op jit(solution)/shard_map/conv_general_dilated | solution.py:33
  (212 shorter events, 83.0 us)
Async XLA Ops:
  7.2 239.1 %all-reduce.5.cloned.1.call-start = ((), (), s32[]{:S(2)}) async-start(), calls=%async_computation.6 | async-start | bytes 3538944 | tf_op jit(solution)/shard_map/psum | solution.py:9
  8.0 28.4 %collective-permute-start.1 = (bf16[1,1,128,128]{3,2,1,0:T(8,128)(2,1)S(1)}, bf16[1,1,128,128]{3,2,1,0:T(8,128)(2,1)S(1)}, u32[]{:S(2)}, u32[]{:S(2)}) collective-permute-start(bf16[1,1,128,128]{3,2,1,0:T(8,128)(2,1)S(1)} %get-tuple-element.35), channel_id=1, source_target_pairs={{8,0},{16,8},{24,16},{32,24},{40,32},{48,40},{56,48},{9,1},{17,9},... | collective-permute-start | bytes 98312 | tf_op jit(solution)/shard_map/ppermute | solution.py:22
  9.3 24.7 %collective-permute-start = (bf16[1,1,128,128]{3,2,1,0:T(8,128)(2,1)S(1)}, bf16[1,1,128,128]{3,2,1,0:T(8,128)(2,1)S(1)}, u32[]{:S(2)}, u32[]{:S(2)}) collective-permute-start(bf16[1,1,128,128]{3,2,1,0:T(8,128)(2,1)S(1)} %get-tuple-element.36), channel_id=1, source_target_pairs={{0,8},{8,16},{16,24},{24,32},{32,40},{40,48},{48,56},{1,9},{9,17},... | collective-permute-start | bytes 98312 | tf_op jit(solution)/shard_map/ppermute | solution.py:19
  16.1 25.0 %collective-permute-start.13 = (bf16[1,1,128,128]{3,2,1,0:T(8,128)(2,1)S(1)}, bf16[1,1,128,128]{3,2,1,0:T(8,128)(2,1)S(1)}, u32[]{:S(2)}, u32[]{:S(2)}) collective-permute-start(bf16[1,1,128,128]{3,2,1,0:T(8,128)(2,1)S(1)} %get-tuple-element.33), channel_id=1, source_target_pairs={{8,0},{16,8},{24,16},{32,24},{40,32},{48,40},{56,48},{9,1},{17,9},... | collective-permute-start | bytes 98312 | tf_op jit(solution)/shard_map/ppermute | solution.py:22
  17.4 19.1 %collective-permute-start.12 = (bf16[1,1,128,128]{3,2,1,0:T(8,128)(2,1)S(1)}, bf16[1,1,128,128]{3,2,1,0:T(8,128)(2,1)S(1)}, u32[]{:S(2)}, u32[]{:S(2)}) collective-permute-start(bf16[1,1,128,128]{3,2,1,0:T(8,128)(2,1)S(1)} %get-tuple-element.34), channel_id=1, source_target_pairs={{0,8},{8,16},{16,24},{24,32},{32,40},{40,48},{48,56},{1,9},{9,17},... | collective-permute-start | bytes 98312 | tf_op jit(solution)/shard_map/ppermute | solution.py:19
  41.2 11.2 %collective-permute-start.14 = (bf16[1,82,1,128]{3,2,1,0:T(2,128)(2,1)S(1)}, bf16[1,82,1,128]{3,2,1,0:T(2,128)(2,1)S(1)}, u32[]{:S(2)}, u32[]{:S(2)}) collective-permute-start(bf16[1,82,1,128]{3,2,1,0:T(2,128)(2,1)S(1)} %get-tuple-element.29), channel_id=1, source_target_pairs={{0,1},{1,2},{2,3},{3,4},{4,5},{5,6},{6,7},{7,0},{8,9},{9,10},{10,1... | collective-permute-start | bytes 62984 | tf_op jit(solution)/shard_map/ppermute | solution.py:19
  41.3 11.1 %collective-permute-start.15 = (bf16[1,82,1,128]{3,2,1,0:T(2,128)(2,1)S(1)}, bf16[1,82,1,128]{3,2,1,0:T(2,128)(2,1)S(1)}, u32[]{:S(2)}, u32[]{:S(2)}) collective-permute-start(bf16[1,82,1,128]{3,2,1,0:T(2,128)(2,1)S(1)} %get-tuple-element.30), channel_id=1, source_target_pairs={{1,0},{2,1},{3,2},{4,3},{5,4},{6,5},{7,6},{0,7},{9,8},{10,9},{11,1... | collective-permute-start | bytes 62984 | tf_op jit(solution)/shard_map/ppermute | solution.py:22
  60.4 18.5 %collective-permute-start.4 = (bf16[1,1,64,128]{3,2,1,0:T(8,128)(2,1)S(1)}, bf16[1,1,64,128]{3,2,1,0:T(8,128)(2,1)S(1)}, u32[]{:S(2)}, u32[]{:S(2)}) collective-permute-start(bf16[1,1,64,128]{3,2,1,0:T(8,128)(2,1)S(1)} %slice.150), channel_id=1, source_target_pairs={{0,8},{8,16},{16,24},{24,32},{32,40},{40,48},{48,56},{1,9},{9,17},... | collective-permute-start | bytes 49160 | tf_op jit(solution)/shard_map/ppermute | solution.py:19
  66.8 12.1 %collective-permute-start.5 = (bf16[1,1,64,128]{3,1,2,0:T(2,128)(2,1)S(1)}, bf16[1,1,64,128]{3,1,2,0:T(2,128)(2,1)S(1)}, u32[]{:S(2)}, u32[]{:S(2)}) collective-permute-start(bf16[1,1,64,128]{3,1,2,0:T(2,128)(2,1)S(1)} %slice.153), channel_id=1, source_target_pairs={{8,0},{16,8},{24,16},{32,24},{40,32},{48,40},{56,48},{9,1},{17,9},... | collective-permute-start | bytes 49160 | tf_op jit(solution)/shard_map/ppermute | solution.py:22
  79.7 10.5 %collective-permute-start.6 = (bf16[1,42,1,128]{3,1,2,0:T(8,128)(2,1)S(1)}, bf16[1,42,1,128]{3,1,2,0:T(8,128)(2,1)S(1)}, u32[]{:S(2)}, u32[]{:S(2)}) collective-permute-start(bf16[1,42,1,128]{3,1,2,0:T(8,128)(2,1)S(1)} %get-tuple-element.55), channel_id=1, source_target_pairs={{0,1},{1,2},{2,3},{3,4},{4,5},{5,6},{6,7},{7,0},{8,9},{9,10},{10,1... | collective-permute-start | bytes 32264 | tf_op jit(solution)/shard_map/ppermute | solution.py:19
  79.8 10.5 %collective-permute-start.7 = (bf16[1,42,1,128]{3,1,2,0:T(8,128)(2,1)S(1)}, bf16[1,42,1,128]{3,1,2,0:T(8,128)(2,1)S(1)}, u32[]{:S(2)}, u32[]{:S(2)}) collective-permute-start(bf16[1,42,1,128]{3,1,2,0:T(8,128)(2,1)S(1)} %get-tuple-element.56), channel_id=1, source_target_pairs={{1,0},{2,1},{3,2},{4,3},{5,4},{6,5},{7,6},{0,7},{9,8},{10,9},{11,1... | collective-permute-start | bytes 32264 | tf_op jit(solution)/shard_map/ppermute | solution.py:22
  102.7 38.8 %collective-permute-start.8 = (bf16[1,1,64,128]{3,0,2,1:T(2,128)(2,1)}, bf16[1,1,64,128]{3,0,2,1:T(2,128)(2,1)}, u32[]{:S(2)}, u32[]{:S(2)}) collective-permute-start(bf16[1,1,64,128]{3,0,2,1:T(2,128)(2,1)} %slice.156), channel_id=1, source_target_pairs={{0,8},{8,16},{16,24},{24,32},{32,40},{40,48},{48,56},{1,9},{9,17},... | collective-permute-start | bytes 49160 | tf_op jit(solution)/shard_map/ppermute | solution.py:19
  109.4 34.4 %collective-permute-start.9 = (bf16[1,1,64,128]{3,0,2,1:T(2,128)(2,1)}, bf16[1,1,64,128]{3,0,2,1:T(2,128)(2,1)S(1)}, u32[]{:S(2)}, u32[]{:S(2)}) collective-permute-start(bf16[1,1,64,128]{3,0,2,1:T(2,128)(2,1)} %slice.159), channel_id=1, source_target_pairs={{8,0},{16,8},{24,16},{32,24},{40,32},{48,40},{56,48},{9,1},{17,9},... | collective-permute-start | bytes 49160 | tf_op jit(solution)/shard_map/ppermute | solution.py:22
  111.3 16.7 %collective-permute-start.16 = (bf16[1,1,64,128]{3,2,1,0:T(8,128)(2,1)}, bf16[1,1,64,128]{3,2,1,0:T(8,128)(2,1)S(1)}, u32[]{:S(2)}, u32[]{:S(2)}) collective-permute-start(bf16[1,1,64,128]{3,2,1,0:T(8,128)(2,1)} %slice.166), channel_id=1, source_target_pairs={{0,8},{8,16},{16,24},{24,32},{32,40},{40,48},{48,56},{1,9},{9,17},... | collective-permute-start | bytes 49160 | tf_op jit(solution)/shard_map/ppermute | solution.py:19
  117.4 10.6 %collective-permute-start.17 = (bf16[1,1,64,128]{3,1,2,0:T(2,128)(2,1)S(1)}, bf16[1,1,64,128]{3,1,2,0:T(2,128)(2,1)S(1)}, u32[]{:S(2)}, u32[]{:S(2)}) collective-permute-start(bf16[1,1,64,128]{3,1,2,0:T(2,128)(2,1)S(1)} %slice.169), channel_id=1, source_target_pairs={{8,0},{16,8},{24,16},{32,24},{40,32},{48,40},{56,48},{9,1},{17,9},... | collective-permute-start | bytes 49160 | tf_op jit(solution)/shard_map/ppermute | solution.py:22
  141.5 235.2 %reduce-scatter.8.cloned.1.call-start = ((), (), s32[]{:S(2)}) async-start(), calls=%async_computation.5 | async-start | bytes 442368 | tf_op jit(solution)/shard_map/reduce_scatter | solution.py:116
  143.9 13.2 %collective-permute-start.10 = (bf16[1,42,1,128]{3,0,2,1:T(2,128)(2,1)S(1)}, bf16[1,42,1,128]{3,0,2,1:T(2,128)(2,1)S(1)}, u32[]{:S(2)}, u32[]{:S(2)}) collective-permute-start(bf16[1,42,1,128]{3,0,2,1:T(2,128)(2,1)S(1)} %get-tuple-element.39), channel_id=1, source_target_pairs={{0,1},{1,2},{2,3},{3,4},{4,5},{5,6},{6,7},{7,0},{8,9},{9,10},{10,1... | collective-permute-start | bytes 32264 | tf_op jit(solution)/shard_map/ppermute | solution.py:19
  144.2 13.0 %collective-permute-start.11 = (bf16[1,42,1,128]{3,0,2,1:T(2,128)(2,1)S(1)}, bf16[1,42,1,128]{3,0,2,1:T(2,128)(2,1)S(1)}, u32[]{:S(2)}, u32[]{:S(2)}) collective-permute-start(bf16[1,42,1,128]{3,0,2,1:T(2,128)(2,1)S(1)} %get-tuple-element.40), channel_id=1, source_target_pairs={{1,0},{2,1},{3,2},{4,3},{5,4},{6,5},{7,6},{0,7},{9,8},{10,9},{11,1... | collective-permute-start | bytes 32264 | tf_op jit(solution)/shard_map/ppermute | solution.py:22
  149.8 11.3 %collective-permute-start.20 = (bf16[1,1,64,128]{3,0,2,1:T(2,128)(2,1)S(1)}, bf16[1,1,64,128]{3,0,2,1:T(2,128)(2,1)S(1)}, u32[]{:S(2)}, u32[]{:S(2)}) collective-permute-start(bf16[1,1,64,128]{3,0,2,1:T(2,128)(2,1)S(1)} %slice.172), channel_id=1, source_target_pairs={{0,8},{8,16},{16,24},{24,32},{32,40},{40,48},{48,56},{1,9},{9,17},... | collective-permute-start | bytes 49160 | tf_op jit(solution)/shard_map/ppermute | solution.py:19
  155.8 166.3 %collective-permute-start.21 = (bf16[1,1,64,128]{3,0,2,1:T(2,128)(2,1)S(1)}, bf16[1,1,64,128]{3,0,2,1:T(2,128)(2,1)S(1)}, u32[]{:S(2)}, u32[]{:S(2)}) collective-permute-start(bf16[1,1,64,128]{3,0,2,1:T(2,128)(2,1)S(1)} %slice.175), channel_id=1, source_target_pairs={{8,0},{16,8},{24,16},{32,24},{40,32},{48,40},{56,48},{9,1},{17,9},... | collective-permute-start | bytes 49160 | tf_op jit(solution)/shard_map/ppermute | solution.py:22
  318.5 59.8 %reduce-scatter.6.cloned.1.call-start = ((), (), s32[]{:S(2)}) async-start(), calls=%async_computation.4 | async-start | bytes 442368 | tf_op jit(solution)/shard_map/reduce_scatter | solution.py:113
  323.6 27.2 %collective-permute-start.22 = (bf16[1,42,1,128]{3,0,2,1:T(2,128)(2,1)S(1)}, bf16[1,42,1,128]{3,0,2,1:T(2,128)(2,1)S(1)}, u32[]{:S(2)}, u32[]{:S(2)}) collective-permute-start(bf16[1,42,1,128]{3,0,2,1:T(2,128)(2,1)S(1)} %get-tuple-element.37), channel_id=1, source_target_pairs={{0,1},{1,2},{2,3},{3,4},{4,5},{5,6},{6,7},{7,0},{8,9},{9,10},{10,1... | collective-permute-start | bytes 32264 | tf_op jit(solution)/shard_map/ppermute | solution.py:19
  323.7 27.1 %collective-permute-start.23 = (bf16[1,42,1,128]{3,0,2,1:T(2,128)(2,1)S(1)}, bf16[1,42,1,128]{3,0,2,1:T(2,128)(2,1)S(1)}, u32[]{:S(2)}, u32[]{:S(2)}) collective-permute-start(bf16[1,42,1,128]{3,0,2,1:T(2,128)(2,1)S(1)} %get-tuple-element.38), channel_id=1, source_target_pairs={{1,0},{2,1},{3,2},{4,3},{5,4},{6,5},{7,6},{0,7},{9,8},{10,9},{11,1... | collective-permute-start | bytes 32264 | tf_op jit(solution)/shard_map/ppermute | solution.py:22
  327.8 52.2 %reduce-scatter.4.cloned.1.call-start = ((), (), s32[]{:S(2)}) async-start(), calls=%async_computation.3 | async-start | bytes 442368 | tf_op jit(solution)/shard_map/reduce_scatter | solution.py:110
  (36 other events, 483.5 us)
Sparse Core Ops, SparseCore 0:
  141.6 104.5 all-reduce.4
  318.6 7.9 reduce-scatter.7
  329.6 11.7 reduce-scatter.5
  353.9 5.8 reduce-scatter.3
